TPU v7x, 256 devices: a whole 4x4x8 slice. The times are simulated.
256 devices in a mesh: ep: 32 (over z, y), tp: 8 (over x, core).
Axes of the slice: x: 4, y: 4, z: 8, core: 2. Of those that a mesh axis runs over, the one named last changes fastest.
Arguments:
- tokens: bfloat16 [1024, 6144], P('ep', 'tp'), may hold values from -6 to 6
- expert_ids: int32 [1024, 2], P('ep'), may hold values from 0 to 7, all different within a row; in each aligned block of 32 rows (0 to 31, 32 to 63, ...) at most 16 rows name the same one
- combine_weights: float32 [1024, 2], P('ep'), may hold values from 0.1 to 1
- gate_codes: bfloat16 [6144, 65536], P(None, ('ep', 'tp')), may hold values from -6 to 6, as said below
- gate_scales: bfloat16 [192, 65536], P(None, ('ep', 'tp')), as said below
- up_codes: bfloat16 [6144, 65536], P(None, ('ep', 'tp')), may hold values from -6 to 6, as said below
- up_scales: bfloat16 [192, 65536], P(None, ('ep', 'tp')), as said below
- down_codes: bfloat16 [65536, 6144], P(('ep', 'tp')), may hold values from -6 to 6, as said below
- down_scales: bfloat16 [2048, 6144], P(('ep', 'tp')), as said below
Outputs:
- mixed: bfloat16 [1024, 6144], P('ep', 'tp')
Inputs may be any that keep to these rules, and one draw needn't show every extreme that they name: `expert_ids`: each token names 2 different experts. Among the 32 tokens of one index of ep no expert is named more than 16 times, a bound that some block reaches. `gate_codes`: every entry is one of 0, 0.5, 1, 1.5, 2, 3, 4, 6 or its negative. `up_codes`: every entry is one of 0, 0.5, 1, 1.5, 2, 3, 4, 6 or its negative. `down_codes`: every entry is one of 0, 0.5, 1, 1.5, 2, 3, 4, 6 or its negative. `gate_scales`: every entry is a power of two. `up_scales`: every entry is a power of two. `down_scales`: every entry is a power of two.
All inputs are finite; a program needn't handle non-finite values.
Results may differ from a plain program's by a relative error of at most 0.014.
Values may be sent and summed in bfloat16 or wider, within the bound.
A program may use at most 128 MiB of HBM per device.

v0:
```python
import jax
import jax.numpy as jnp
from jax import lax
from jax.sharding import PartitionSpec as P

EXPERTS = 8
CAP = 16


def dequant(code_values, scales):
    count_in, count_out = code_values.shape
    blocks = code_values.reshape(count_in // 32, 32, count_out) * scales[:, None, :]
    return blocks.reshape(count_in, count_out)


def slot_targets(expert_ids):
    count_tokens, count_top = expert_ids.shape
    flat_ids = expert_ids.reshape(-1)
    is_expert = (flat_ids[:, None] == jnp.arange(EXPERTS, dtype=jnp.int32)[None, :]).astype(
        jnp.int32
    )
    before = jnp.cumsum(is_expert, axis=0) - is_expert
    slot_rank = jnp.sum(before * is_expert, axis=1)
    return (flat_ids * CAP + slot_rank).reshape(count_tokens, count_top)


def per_device(
    tokens,
    expert_ids,
    combine_weights,
    gate_codes,
    gate_scales,
    up_codes,
    up_scales,
    down_codes,
    down_scales,
):
    owners = lax.axis_size("ep") // EXPERTS
    gate_matrix = dequant(gate_codes, gate_scales)
    up_matrix = dequant(up_codes, up_scales)
    down_matrix = dequant(down_codes, down_scales)
    target = slot_targets(expert_ids)
    slot_index = jnp.arange(EXPERTS * CAP, dtype=jnp.int32)
    chosen = jnp.zeros((EXPERTS * CAP, target.shape[0]), jnp.float32)
    weighting = jnp.zeros((target.shape[0], EXPERTS * CAP), jnp.float32)
    for column in range(target.shape[1]):
        match_rows = target[:, column][:, None] == slot_index[None, :]
        weighting = weighting + combine_weights[:, column][:, None] * match_rows.astype(jnp.float32)
        chosen = chosen + jnp.transpose(match_rows).astype(jnp.float32)
    chosen = chosen.astype(jnp.bfloat16)
    packed = jnp.dot(chosen, tokens, preferred_element_type=jnp.float32).astype(jnp.bfloat16)
    packed = packed.reshape(EXPERTS, CAP, tokens.shape[1])
    slot_rows = lax.all_gather(
        lax.all_to_all(
            jnp.repeat(packed, owners, axis=0), "ep", split_axis=0, concat_axis=0, tiled=True
        ),
        "tp",
        axis=2,
        tiled=True,
    )
    count_src, count_slots, model_width = slot_rows.shape
    flat_rows = slot_rows.reshape(count_src * count_slots, model_width)
    gate_proj = jnp.dot(flat_rows, gate_matrix, preferred_element_type=jnp.float32)
    up_proj = jnp.dot(flat_rows, up_matrix, preferred_element_type=jnp.float32)
    hidden = (jax.nn.silu(gate_proj) * up_proj).astype(jnp.bfloat16)
    partial_value = jnp.dot(hidden, down_matrix, preferred_element_type=jnp.float32).astype(
        jnp.bfloat16
    )
    partial_value = partial_value.reshape(count_src, count_slots, model_width)
    reduced = lax.psum_scatter(
        partial_value.astype(jnp.float32).astype(jnp.bfloat16),
        "tp",
        scatter_dimension=2,
        tiled=True,
    ).astype(jnp.float32)
    returned = lax.all_to_all(
        reduced.astype(jnp.bfloat16), "ep", split_axis=0, concat_axis=0, tiled=True
    ).astype(reduced.dtype)
    feature_width = returned.shape[2]
    grouped = returned.reshape(EXPERTS, owners, CAP, feature_width)
    per_expert = jnp.sum(grouped, axis=1).reshape(EXPERTS * CAP, feature_width)
    mixed_out = jnp.dot(weighting, per_expert, preferred_element_type=jnp.float32)
    return mixed_out.astype(jnp.bfloat16)


def solution(mesh):
    placed = (
        P("ep", "tp"),
        P("ep", None),
        P("ep", None),
        P(None, ("ep", "tp")),
        P(None, ("ep", "tp")),
        P(None, ("ep", "tp")),
        P(None, ("ep", "tp")),
        P(("ep", "tp"), None),
        P(("ep", "tp"), None),
    )
    return jax.shard_map(
        per_device, mesh=mesh, in_specs=placed, out_specs=P("ep", "tp"), check_vma=False
    )
```

profile of v0, /device:TPU:1, one launch (start us, length us, event | category | flops | bytes accessed | tf_op | source)
XLA Modules:
  0.0 186.8 jit_solution(12755171529070535130)
XLA Ops:
  6.5 0.0 copy-start
  6.5 0.0 copy-start.1
  6.5 0.0 copy-start.4
  6.5 0.0 all-gather.2.cloned.1.call-start
  6.5 0.9 copy.16
  7.5 0.1 eq.59
  7.6 0.1 fusion.9
  7.6 0.1 reduce_window_sum.11
  7.7 0.2 select_reduce_fusion
  7.9 0.1 reduce_sum.21
  8.0 0.1 copy.17
  8.1 0.7 multiply_add_fusion
  8.8 0.0 copy-done
  8.8 0.2 convolution_convert_fusion.1
  9.0 0.1 broadcast_in_dim.2
  9.1 33.0 %all_to_all.10 = bf16[32,16,768]{2,1,0:T(8,128)(2,1)} all-to-all(bf16[32,16,768]{2,1,0:T(8,128)(2,1)S(1)} %bitcast.30), channel_id=1, replica_groups=mesh['ep'=32,'tp'=8] {'ep'}, dimensions={0} | all-to-all | bytes 1572864 | tf_op jit(solution)/shard_map/all_to_all | solution.py:54
  42.1 0.0 all-gather.2.cloned.1.call-update
  42.1 0.0 copy-start.5
  42.1 0.0 reduce-scatter.2.cloned.1.call-start
  42.2 0.0 copy-done.1
  42.2 0.0 copy-done.4
  42.2 0.0 copy-start.2
  42.2 1.9 %bitcast_multiply_fusion.2 = bf16[6144,256]{1,0:T(8,128)(2,1)} fusion(bf16[6144,256]{1,0:T(8,128)(2,1)S(1)} %copy-done.1, bf16[192,256]{1,0:T(8,128)(2,1)S(1)} %copy-done.4), kind=kLoop, calls=%fused_computation.3 | loop fusion | flops 1572864 | bytes 6389760 | tf_op jit(solution)/shard_map/mul | solution.py:12
  44.1 0.0 copy-done.5
  44.1 1.1 copy-done.2
  45.2 0.0 copy-start.3
  45.2 0.0 copy-start.6
  45.2 0.3 bitcast_multiply_fusion
  45.5 1.6 copy-done.3
  47.1 0.0 copy-done.6
  47.1 1.9 %bitcast_multiply_fusion.1 = bf16[6144,256]{1,0:T(8,128)(2,1)} fusion(bf16[6144,256]{1,0:T(8,128)(2,1)S(1)} %copy-done.3, bf16[192,256]{1,0:T(8,128)(2,1)S(1)} %copy-done.6), kind=kLoop, calls=%fused_computation.2 | loop fusion | flops 1572864 | bytes 6389760 | tf_op jit(solution)/shard_map/mul | solution.py:12
  49.0 35.7 %all-gather.2.cloned.1.call-done = bf16[32,16,6144]{2,1,0:T(8,128)(2,1)} async-done(((bf16[32,16,768]{2,1,0:T(8,128)(2,1)}), bf16[32,16,6144]{2,1,0:T(8,128)(2,1)}) %all-gather.2.cloned.1.call-update) | async-done | bytes 6291472 | tf_op jit(solution)/shard_map/all_gather | solution.py:53
  84.7 6.3 %fusion.20 = f32[512,256]{1,0:T(8,128)} fusion(bf16[512,6144]{1,0:T(8,128)(2,1)} %bitcast.33, bf16[6144,256]{1,0:T(8,128)(2,1)} %bitcast_multiply_fusion.2), kind=kOutput, calls=%fused_computation.40 | convolution fusion | flops 1610612736 | bytes 9961472 | tf_op jit(solution)/shard_map/dot_general | solution.py:63
  91.0 13.1 %convolution_convert_fusion = bf16[512,6144]{1,0:T(8,128)(2,1)} fusion(bf16[256,6144]{1,0:T(8,128)(2,1)S(1)} %bitcast_multiply_fusion, bf16[512,6144]{1,0:T(8,128)(2,1)} %bitcast.34, bf16[6144,256]{1,0:T(8,128)(2,1)} %bitcast_multiply_fusion.1, f32[512,256]{1,0:T(8,128)} %fusion.20), kind=kOutput, calls=%fused_computation | convolution fusion | flops 3225157632 | bytes 19398656 | tf_op jit(solution)/shard_map/dot_general | solution.py:66
  104.1 0.0 copy-start.7
  104.1 0.0 reduce-scatter.2.cloned.1.call-update
  104.1 44.3 %reduce-scatter.2.cloned.1.call-done = bf16[32,16,768]{2,1,0:T(8,128)(2,1)} async-done(((bf16[32,16,6144]{2,1,0:T(8,128)(2,1)}), bf16[32,16,768]{2,1,0:T(8,128)(2,1)}) %reduce-scatter.2.cloned.1.call-update) | async-done | bytes 786448 | tf_op jit(solution)/shard_map/reduce_scatter | solution.py:70
  148.5 9.6 %all-to-all-start.1 = ((bf16[32,16,768]{2,1,0:T(8,128)(2,1)}), bf16[32,16,768]{2,1,0:T(8,128)(2,1)S(1)}, u32[]{:S(2)}, u32[]{:S(2)}) async-start(bf16[32,16,768]{2,1,0:T(8,128)(2,1)} %reduce-scatter.2.cloned.1.call-done), calls=%async_computation.2 | async-start | bytes 1572864 | tf_op jit(solution)/shard_map/all_to_all | solution.py:76
  158.1 0.0 copy-done.7
  158.1 20.9 %all-to-all-done.1 = bf16[32,16,768]{2,1,0:T(8,128)(2,1)S(1)} async-done(((bf16[32,16,768]{2,1,0:T(8,128)(2,1)}), bf16[32,16,768]{2,1,0:T(8,128)(2,1)S(1)}, u32[]{:S(2)}, u32[]{:S(2)}) %all-to-all-start.1) | async-done | bytes 786464 | tf_op jit(solution)/shard_map/all_to_all | solution.py:76
  179.0 0.1 convert_reduce_fusion
  179.1 0.8 convolution_convert_fusion.2
  (2 shorter events, 0.0 us)
Async XLA Ops:
  6.5 2.3 %copy-start = (bf16[32,768]{1,0:T(8,128)(2,1)S(1)}, bf16[32,768]{1,0:T(8,128)(2,1)}, u32[]{:S(2)}) copy-start(bf16[32,768]{1,0:T(8,128)(2,1)} %param.9) | copy-start | bytes 147460
  6.5 35.6 %copy-start.1 = (bf16[6144,256]{1,0:T(8,128)(2,1)S(1)}, bf16[6144,256]{1,0:T(8,128)(2,1)}, u32[]{:S(2)}) copy-start(bf16[6144,256]{1,0:T(8,128)(2,1)} %param.12) | copy-start | bytes 9437188
  6.5 35.6 %copy-start.4 = (bf16[192,256]{1,0:T(8,128)(2,1)S(1)}, bf16[192,256]{1,0:T(8,128)(2,1)}, u32[]{:S(2)}) copy-start(bf16[192,256]{1,0:T(8,128)(2,1)} %param.13) | copy-start | bytes 294916
  6.5 78.2 %all-gather.2.cloned.1.call-start = ((), (), s32[]{:S(2)}) async-start(), calls=%async_computation.3 | async-start | bytes 7077888 | tf_op jit(solution)/shard_map/all_gather | solution.py:53
  42.1 2.0 %copy-start.5 = (bf16[8,6144]{1,0:T(8,128)(2,1)S(1)}, bf16[8,6144]{1,0:T(8,128)(2,1)}, u32[]{:S(2)}) copy-start(bf16[8,6144]{1,0:T(8,128)(2,1)} %param.17) | copy-start | bytes 294916
  42.1 106.4 %reduce-scatter.2.cloned.1.call-start = ((), (), s32[]{:S(2)}) async-start(), calls=%async_computation.4 | async-start | bytes 7077888 | tf_op jit(solution)/shard_map/reduce_scatter | solution.py:70
  42.2 3.0 %copy-start.2 = (bf16[256,6144]{1,0:T(8,128)(2,1)S(1)}, bf16[256,6144]{1,0:T(8,128)(2,1)}, u32[]{:S(2)}) copy-start(bf16[256,6144]{1,0:T(8,128)(2,1)} %param.16) | copy-start | bytes 9437188
  45.2 1.9 %copy-start.3 = (bf16[6144,256]{1,0:T(8,128)(2,1)S(1)}, bf16[6144,256]{1,0:T(8,128)(2,1)}, u32[]{:S(2)}) copy-start(bf16[6144,256]{1,0:T(8,128)(2,1)} %param.14) | copy-start | bytes 9437188
  45.2 1.9 %copy-start.6 = (bf16[192,256]{1,0:T(8,128)(2,1)S(1)}, bf16[192,256]{1,0:T(8,128)(2,1)}, u32[]{:S(2)}) copy-start(bf16[192,256]{1,0:T(8,128)(2,1)} %param.15) | copy-start | bytes 294916
  104.1 53.9 %copy-start.7 = (f32[32,2]{0,1:T(2,128)S(1)}, f32[32,2]{0,1:T(2,128)}, u32[]{:S(2)}) copy-start(f32[32,2]{0,1:T(2,128)} %param.11) | copy-start | bytes 772
  148.5 30.5 %all-to-all-start.1 = ((bf16[32,16,768]{2,1,0:T(8,128)(2,1)}), bf16[32,16,768]{2,1,0:T(8,128)(2,1)S(1)}, u32[]{:S(2)}, u32[]{:S(2)}) async-start(bf16[32,16,768]{2,1,0:T(8,128)(2,1)} %reduce-scatter.2.cloned.1.call-done), calls=%async_computation.2 | async-start | bytes 1572864 | tf_op jit(solution)/shard_map/all_to_all | solution.py:76
Sparse Core Ops, SparseCore 0:
  42.2 42.4 all-gather.1
  104.3 44.1 reduce-scatter.1
where the time goes:
time: 188 us; the launch traced here: 187 us
  waiting for transfers between devices  101 us (54%)
  blocking collectives  33 us (18%)
  matrix products  20.4 us (11%)
  between operations  13.5 us (7%)
  starting transfers between devices  9.61 us (5%)
  other arithmetic  5.26 us (3%)
  local copies, waits for them, and re-layouts  3.99 us (2%)
    reduce_scatter x1, waiting for transfers between devices, per_device(): lax.psum_scatter(partial_value.astype(jnp.float32).astype(jnp.bfloat16),...  44.3 us
    all_gather x1, waiting for transfers between devices, per_device(): lax.all_gather(lax.all_to_all(jnp.repeat(packed, owners, axis=0), 'ep', s...  35.7 us
    all_to_all x1, blocking collectives, per_device(): lax.all_to_all(jnp.repeat(packed, owners, axis=0), 'ep', split_axis=0, co...  33 us
    all_to_all x1, waiting for transfers between devices, per_device(): lax.all_to_all(reduced.astype(jnp.bfloat16), 'ep', split_axis=0, concat_a...  20.9 us
    dot_general x1, matrix products, per_device(): jnp.dot(hidden, down_matrix, preferred_element_type=jnp.float32)  13.1 us
    all_to_all x1, starting transfers between devices, per_device(): lax.all_to_all(reduced.astype(jnp.bfloat16), 'ep', split_axis=0, concat_a...  9.57 us
    dot_general x1, matrix products, per_device(): jnp.dot(flat_rows, gate_matrix, preferred_element_type=jnp.float32)  6.3 us
    mul x3, other arithmetic, dequant(): code_values.reshape(count_in // 32, 32, count_out) * scales[:, None, :]  4.1 us
  transfers between devices with their start and end apart: 3, of which 3 were waited for; matrix products, arithmetic and copies ran while one was open for 2% of the time, Pallas kernels for 0%

commit v1 on v0

v1 whole, which is shorter than its diff:
```python
import functools

import jax
import jax.numpy as jnp
from jax import lax
from jax.experimental import pallas as pl
from jax.experimental.pallas import tpu as pltpu
from jax.sharding import PartitionSpec as P

EXPERTS = 8
CAP = 16
NX, NY, NZ = 4, 4, 8
MESH = pl.DeviceIdType.MESH
BF, F32 = jnp.bfloat16, jnp.float32


def mult(value, factor):
    return pl.multiple_of(value, factor)


def kernel(
    tokens, ids, combine, gate_c, gate_s, up_c, up_s, down_c, down_s,
    out,
    packed, X, PS, H, FIN, YB, WMAT, RA, RB, RA2, RB2,
    GC, GS, UC, US, DC, DS,
    wl_sem, ws_sem, wr_sem, zs_sem, zr_sem, zl_sem,
    as_sem, ar_sem, bs_sem, br_sem,
    rs_send, rs_recv, fs_sem, fr_sem,
):
    ep, tp = lax.axis_index("ep"), lax.axis_index("tp")
    z, y = ep // NY, lax.rem(ep, NY)
    x, c = tp // 2, lax.rem(tp, 2)
    feat = tokens.shape[1]
    wide = 2 * feat
    parity = lax.rem(z, 2)
    xs = [lax.rem(x + d, NX) for d in range(NX)]
    ys = [lax.rem(y + d, NY) for d in range(NY)]

    def dev(zz, yy, xx, cc):
        return (zz * NY + yy, xx * 2 + cc)

    dev_x = {1: dev(z, y, xs[1], c), -1: dev(z, y, xs[3], c)}
    dev_y = {1: dev(z, ys[1], x, c), -1: dev(z, ys[3], x, c)}
    partner = dev(z, y, x, 1 - c)

    barrier = pltpu.get_barrier_semaphore()
    greeted = [partner, dev_x[1], dev_x[-1], dev_y[1], dev_y[-1]]
    for dz in range(1, NZ):
        zt = lax.rem(z + dz, NZ)
        greeted += [dev(zt, y, x, c), dev(zt, y, x, 1 - c)]
    for who in greeted:
        pl.semaphore_signal(barrier, inc=1, device_id=who, device_id_type=MESH)

    weights = [(gate_c, GC), (gate_s, GS), (up_c, UC), (up_s, US), (down_c, DC), (down_s, DS)]
    local_w = []
    for i, (src, dst) in enumerate(weights):
        copy = pltpu.make_async_copy(src, dst.at[0], wl_sem.at[i])
        copy.start()
        local_w.append(copy)

    count = ids.shape[1]
    slot = lax.broadcasted_iota(jnp.int32, (EXPERTS * CAP, count), 0)
    expert, rank = slot // CAP, lax.rem(slot, CAP)
    first = ids[0:1, :] == expert
    second = ids[1:2, :] == expert
    member = jnp.logical_or(first, second)
    before = (
        lax.broadcasted_iota(jnp.int32, (count, count), 0)
        < lax.broadcasted_iota(jnp.int32, (count, count), 1)
    )
    member_rank = jnp.dot(
        member.astype(F32).astype(BF), before.astype(F32).astype(BF), preferred_element_type=F32
    )
    chosen = jnp.logical_and(member, member_rank == rank.astype(F32))
    packed[...] = jnp.dot(
        chosen.astype(F32).astype(BF), tokens[...], preferred_element_type=F32
    ).astype(BF)
    WMAT[...] = jnp.where(
        chosen, jnp.where(first, combine[0:1, :], combine[1:2, :]), 0.0
    )

    pl.semaphore_wait(barrier, len(greeted))

    z_row = mult(y * 64 + (z // 2) * 16, 16)
    z_col = mult(x * wide + c * feat, 128)
    z_idx = (z // 2) * 2 + c
    at_home = c == parity
    z_sends = []
    for dz in (4, 3, 5, 2, 6, 1, 7, 0):
        zt = lax.rem(z + dz, NZ)
        z_sends.append((dz, pltpu.make_async_remote_copy(
            src_ref=packed.at[pl.ds(mult(zt * CAP, CAP), CAP), :],
            dst_ref=X.at[pl.ds(z_row, CAP), pl.ds(z_col, feat)],
            send_sem=zs_sem.at[dz],
            recv_sem=zr_sem.at[z_idx],
            device_id=dev(zt, y, x, parity),
            device_id_type=MESH,
        )))
    for dz, copy in z_sends:
        if dz == 0:
            pl.when(jnp.logical_not(at_home))(copy.start)
        else:
            copy.start()
    remote_w = []
    for i, (src, dst) in enumerate(weights):
        copy = pltpu.make_async_remote_copy(
            src_ref=src, dst_ref=dst.at[1], send_sem=ws_sem.at[i], recv_sem=wr_sem.at[i],
            device_id=partner, device_id_type=MESH,
        )
        copy.start()
        remote_w.append(copy)

    @pl.when(at_home)
    def _():
        copy = pltpu.make_async_copy(
            packed.at[pl.ds(mult(z * CAP, CAP), CAP), :],
            X.at[pl.ds(z_row, CAP), pl.ds(z_col, feat)],
            zl_sem,
        )
        copy.start()
        copy.wait()

    def z_arrived(zi):
        for cc in range(2):
            region = X.at[
                pl.ds(mult(y * 64 + zi * 16, 16), CAP),
                pl.ds(mult(x * wide + cc * feat, 128), feat),
            ]
            copy = pltpu.make_async_remote_copy(
                src_ref=region, dst_ref=region, send_sem=zs_sem.at[0],
                recv_sem=zr_sem.at[zi * 2 + cc], device_id=partner, device_id_type=MESH,
            )
            here = jnp.logical_and(2 * zi + c == z, c == cc)
            pl.when(jnp.logical_not(here))(copy.wait_recv)

    def region(ref, half, yy, xx, part):
        start, size = {None: (0, 32), 0: (0, 16), 1: (16, 16)}[part]
        return ref.at[
            pl.ds(mult(yy * 64 + half * 32 + start, 16), size),
            pl.ds(mult(xx * wide, 128), wide),
        ]

    sends = []
    SIGN = (1, -1)

    class Gather:
        def __init__(self, half, send_sem, recv_sem):
            self.half, self.ss, self.rs = half, send_sem, recv_sem
            self.line = ys if half == 0 else xs
            self.other = xs if half == 0 else ys
            self.dev1 = dev_y if half == 0 else dev_x
            self.dev2 = dev_x if half == 0 else dev_y

        def reg(self, a, b, part):
            p, q = self.line[a % 4], self.other[b % 4]
            yy, xx = (p, q) if self.half == 0 else (q, p)
            return region(X, self.half, yy, xx, part)

        def send(self, a, b, part, device, index):
            r = self.reg(a, b, part)
            copy = pltpu.make_async_remote_copy(
                src_ref=r, dst_ref=r, send_sem=self.ss.at[index], recv_sem=self.rs.at[index],
                device_id=device, device_id_type=MESH,
            )
            copy.start()
            sends.append(copy)

        def arrived(self, a, b, part, index):
            r = self.reg(a, b, part)
            pltpu.make_async_remote_copy(
                src_ref=r, dst_ref=r, send_sem=self.ss.at[index], recv_sem=self.rs.at[index],
                device_id=partner, device_id_type=MESH,
            ).wait_recv()

        def start1(self):
            self.send(0, 0, None, self.dev1[1], 0)
            self.send(0, 0, None, self.dev1[-1], 1)

        OFF = (0, -1, 1, 2)

        def start2(self, j):
            self.send(self.OFF[j], 0, None, self.dev2[1], 4 + 4 * j)
            self.send(self.OFF[j], 0, None, self.dev2[-1], 5 + 4 * j)

        def pass1(self):
            self.arrived(-1, 0, None, 0)
            self.send(-1, 0, 0, self.dev1[1], 2)
            self.arrived(1, 0, None, 1)
            self.send(1, 0, 1, self.dev1[-1], 3)

        def end1(self):
            self.arrived(2, 0, 0, 2)
            self.arrived(2, 0, 1, 3)

        def pass2(self, j):
            a = self.OFF[j]
            self.arrived(a, -1, None, 4 + 4 * j)
            self.send(a, -1, 0, self.dev2[1], 6 + 4 * j)
            self.arrived(a, 1, None, 5 + 4 * j)
            self.send(a, 1, 1, self.dev2[-1], 7 + 4 * j)

        def end2(self, j):
            self.arrived(self.OFF[j], 2, 0, 6 + 4 * j)
            self.arrived(self.OFF[j], 2, 1, 7 + 4 * j)

    A, B = Gather(0, as_sem, ar_sem), Gather(1, bs_sem, br_sem)
    z_arrived(0)
    z_arrived(1)
    A.start1()
    z_arrived(2)
    z_arrived(3)
    B.start1()
    A.start2(0)
    B.start2(0)
    for g in (A, B):
        g.pass1()
    for g in (A, B):
        g.start2(1)
        g.start2(2)
    for g in (A, B):
        g.pass2(0)
    for g in (A, B):
        g.end1()
        g.start2(3)
    for j in (1, 2, 3):
        for g in (A, B):
            g.pass2(j)
    for j in range(4):
        for g in (A, B):
            g.end2(j)

    for copy in local_w:
        copy.wait()
    for copy in remote_w:
        copy.wait_recv()

    def scaled(codes, scales):
        rows, cols = codes.shape
        blocks = codes.reshape(rows // 32, 32, cols) * scales[:, None, :]
        return blocks.reshape(rows, cols)

    deep = X.shape[1]
    step = 1536
    for s in range(2):
        gate = up = None
        for k in range(deep // step):
            rows, srows = slice(k * step, (k + 1) * step), slice(k * step // 32, (k + 1) * step // 32)
            xk = X[:, rows]
            g = jnp.dot(xk, scaled(GC[s, rows, :], GS[s, srows, :]), preferred_element_type=F32)
            u = jnp.dot(xk, scaled(UC[s, rows, :], US[s, srows, :]), preferred_element_type=F32)
            gate, up = (g, u) if gate is None else (gate + g, up + u)
        hidden = gate / (1.0 + jnp.exp(-gate)) * up
        H[:, s * 256:(s + 1) * 256] = hidden.astype(BF)

    def project(xx):
        piece = 512
        for i in range(wide // piece):
            cols = pl.ds(mult(xx * wide + i * piece, 128), piece)
            total = None
            for s in range(2):
                part = jnp.dot(
                    H[:, s * 256:(s + 1) * 256], scaled(DC[s, :, cols], DS[s, :, cols]),
                    preferred_element_type=F32,
                )
                total = part if total is None else total + part
            PS[:, cols] = total.astype(BF)

    class Reduce:
        def __init__(self, half, base, R1, R2):
            self.half, self.base, self.R1, self.R2 = half, base, R1, R2
            self.line = xs if half == 0 else ys
            self.other = ys if half == 0 else xs
            self.dev1 = dev_x if half == 0 else dev_y
            self.dev2 = dev_y if half == 0 else dev_x

        def reg(self, a, b, part):
            p, q = self.line[a % 4], self.other[b % 4]
            yy, xx = (q, p) if self.half == 0 else (p, q)
            return region(PS, self.half, yy, xx, part)

        def copy(self, src, dst, device, index):
            return pltpu.make_async_remote_copy(
                src_ref=src, dst_ref=dst, send_sem=rs_send.at[self.base + index],
                recv_sem=rs_recv.at[self.base + index], device_id=device, device_id_type=MESH,
            )

        def send(self, src, dst, device, index):
            copy = self.copy(src, dst, device, index)
            copy.start()
            sends.append(copy)

        def arrived(self, dst, index):
            self.copy(dst, dst, partner, index).wait_recv()

        def far(self, pieces, buf, dev_, index):
            self.send(pieces(2, 0), buf.at[pl.ds(64, 16)], dev_[-1], index)
            self.send(pieces(2, 1), buf.at[pl.ds(80, 16)], dev_[1], index + 1)

        def near(self, pieces, buf, dev_, index):
            self.arrived(buf.at[pl.ds(64, 16)], index)
            low = pieces(-1, 0)
            low[...] = (low[...].astype(F32) + buf[64:80, :].astype(F32)).astype(BF)
            self.send(pieces(-1, None), buf.at[pl.ds(32, 32)], dev_[-1], index + 2)
            self.arrived(buf.at[pl.ds(80, 16)], index + 1)
            high = pieces(1, 1)
            high[...] = (high[...].astype(F32) + buf[80:96, :].astype(F32)).astype(BF)
            self.send(pieces(1, None), buf.at[pl.ds(0, 32)], dev_[1], index + 3)

        def own(self, pieces, buf, index):
            self.arrived(buf.at[pl.ds(32, 32)], index + 2)
            self.arrived(buf.at[pl.ds(0, 32)], index + 3)
            total = pieces(0, None)[...].astype(F32) + buf[0:32, :].astype(F32)
            return (total + buf[32:64, :].astype(F32)).astype(BF)

        OFF = (2, 1, -1, 0)

        def ring1(self, j):
            return (lambda a, part: self.reg(a, self.OFF[j], part)), self.R1.at[j], 4 * j

        def far1(self, j):
            pieces, buf, index = self.ring1(j)
            self.far(pieces, buf, self.dev1, index)

        def near1(self, j):
            pieces, buf, index = self.ring1(j)
            self.near(pieces, buf, self.dev1, index)

        def own1(self, j):
            pieces, buf, index = self.ring1(j)
            value = self.own(pieces, buf, index)
            pieces(0, None)[...] = value

        def ring2(self, a, part):
            return self.reg(0, a, part)

        def far2(self):
            self.far(self.ring2, self.R2, self.dev2, 16)

        def near2(self):
            self.near(self.ring2, self.R2, self.dev2, 16)

        def own2(self):
            FIN[self.half * 32:(self.half + 1) * 32, :] = self.own(self.ring2, self.R2, 16)

    RA_, RB_ = Reduce(0, 0, RA, RA2), Reduce(1, 20, RB, RB2)
    project(xs[2])
    for j in range(4):
        RA_.far1(j)
    RB_.far1(0)
    project(xs[1])
    RB_.far1(1)
    project(xs[3])
    RB_.far1(2)
    project(xs[0])
    RB_.far1(3)
    for j in range(4):
        RA_.near1(j)
        RB_.near1(j)
    for r in (RA_, RB_):
        r.own1(0)
        r.far2()
    for j in (1, 2):
        for r in (RA_, RB_):
            r.own1(j)
    for r in (RA_, RB_):
        r.near2()
    for r in (RA_, RB_):
        r.own1(3)

    returns = []

    def give_back(zi):
        for cc in range(2):
            src = FIN.at[pl.ds(zi * 16, 16), pl.ds(cc * feat, feat)]
            dst = YB.at[pl.ds(mult(z * CAP, CAP), CAP), :]
            copy = pltpu.make_async_remote_copy(
                src_ref=src, dst_ref=dst, send_sem=fs_sem.at[zi * 2 + cc], recv_sem=fr_sem.at[z],
                device_id=dev(2 * zi + c, y, x, cc), device_id_type=MESH,
            )
            here = jnp.logical_and(2 * zi + c == z, c == cc)
            pl.when(jnp.logical_not(here))(copy.start)
            returns.append((here, copy))

            @pl.when(here)
            def _():
                move = pltpu.make_async_copy(src, dst, zl_sem)
                move.start()
                move.wait()

    RA_.own2()
    give_back(0)
    give_back(1)
    RB_.own2()
    give_back(2)
    give_back(3)

    for e in range(EXPERTS):
        dst = YB.at[pl.ds(e * CAP, CAP), :]
        copy = pltpu.make_async_remote_copy(
            src_ref=dst, dst_ref=dst, send_sem=fs_sem.at[0], recv_sem=fr_sem.at[e],
            device_id=partner, device_id_type=MESH,
        )
        here = jnp.logical_and(z == e, at_home)
        pl.when(jnp.logical_not(here))(copy.wait_recv)

    weight = WMAT[...]
    high = weight.astype(BF)
    low = (weight - high.astype(F32)).astype(BF)
    dims = (((0,), (0,)), ((), ()))
    mixed = lax.dot_general(high, YB[...], dims, preferred_element_type=F32)
    mixed = mixed + lax.dot_general(low, YB[...], dims, preferred_element_type=F32)
    out[...] = mixed.astype(BF)

    for copy in remote_w:
        copy.wait_send()
    for dz, copy in z_sends:
        if dz == 0:
            pl.when(jnp.logical_not(at_home))(copy.wait_send)
        else:
            copy.wait_send()
    for copy in sends:
        copy.wait_send()
    for here, copy in returns:
        pl.when(jnp.logical_not(here))(copy.wait_send)


def per_device(tokens, ids, combine, gate_c, gate_s, up_c, up_s, down_c, down_s):
    count, feat = tokens.shape
    deep, units = gate_c.shape
    wide = 2 * feat
    vmem, hbm = pl.BlockSpec(memory_space=pltpu.VMEM), pl.BlockSpec(memory_space=pl.ANY)
    dma = pltpu.SemaphoreType.DMA
    return pl.pallas_call(
        kernel,
        out_shape=jax.ShapeDtypeStruct((count, feat), BF),
        in_specs=[vmem] * 3 + [hbm] * 6,
        out_specs=vmem,
        scratch_shapes=[
            pltpu.VMEM((EXPERTS * CAP, feat), BF),
            pltpu.VMEM((256, deep), BF),
            pltpu.VMEM((256, deep), BF),
            pltpu.VMEM((256, 2 * units), BF),
            pltpu.VMEM((64, wide), BF),
            pltpu.VMEM((EXPERTS * CAP, feat), BF),
            pltpu.VMEM((EXPERTS * CAP, count), F32),
            pltpu.VMEM((4, 96, wide), BF),
            pltpu.VMEM((4, 96, wide), BF),
            pltpu.VMEM((96, wide), BF),
            pltpu.VMEM((96, wide), BF),
            pltpu.VMEM((2,) + gate_c.shape, BF),
            pltpu.VMEM((2,) + gate_s.shape, BF),
            pltpu.VMEM((2,) + up_c.shape, BF),
            pltpu.VMEM((2,) + up_s.shape, BF),
            pltpu.VMEM((2,) + down_c.shape, BF),
            pltpu.VMEM((2,) + down_s.shape, BF),
            dma((6,)), dma((6,)), dma((6,)), dma((8,)), dma((8,)), dma,
            dma((20,)), dma((20,)), dma((20,)), dma((20,)),
            dma((40,)), dma((40,)), dma((8,)), dma((8,)),
        ],
        compiler_params=pltpu.CompilerParams(
            collective_id=0, has_side_effects=True, vmem_limit_bytes=63 * 2**20
        ),
        name="moe",
    )(tokens, jnp.transpose(ids), jnp.transpose(combine), gate_c, gate_s, up_c, up_s, down_c, down_s)


def solution(mesh):
    placed = (
        P("ep", "tp"),
        P("ep", None),
        P("ep", None),
        P(None, ("ep", "tp")),
        P(None, ("ep", "tp")),
        P(None, ("ep", "tp")),
        P(None, ("ep", "tp")),
        P(("ep", "tp"), None),
        P(("ep", "tp"), None),
    )
    return jax.shard_map(
        per_device, mesh=mesh, in_specs=placed, out_specs=P("ep", "tp"), check_vma=False
    )
```

time: 188 us -> 71.4 us (0.38)
  waiting for transfers between devices: 101 us -> 0 us
  Pallas kernels: 0 us -> 69.8 us
  blocking collectives: 33 us -> 0 us
  matrix products: 20.4 us -> 0 us
  between operations: 13.5 us -> 0.01 us
  starting transfers between devices: 9.61 us -> 0 us
  other arithmetic: 5.26 us -> 0 us
  local copies, waits for them, and re-layouts: 3.99 us -> 1.42 us
    pallas_call x0 -> x1, Pallas kernels: none -> 69.8 us  [per_device(): pl.pallas_call(kernel, out_shape=jax.ShapeDtypeStruct((count, feat), BF),...]
    reduce_scatter x1 -> x0, waiting for transfers between devices: 44.3 us -> none  [per_device(): lax.psum_scatter(partial_value.astype(jnp.float32).astype(jnp.bfloat16),...]
    all_gather x1 -> x0, waiting for transfers between devices: 35.7 us -> none  [per_device(): lax.all_gather(lax.all_to_all(jnp.repeat(packed, owners, axis=0), 'ep', s...]
    all_to_all x1 -> x0, blocking collectives: 33 us -> none  [per_device(): lax.all_to_all(jnp.repeat(packed, owners, axis=0), 'ep', split_axis=0, co...]
    all_to_all x1 -> x0, waiting for transfers between devices: 20.9 us -> none  [per_device(): lax.all_to_all(reduced.astype(jnp.bfloat16), 'ep', split_axis=0, concat_a...]
    dot_general x4 -> x0, matrix products: 20.4 us -> none  [the longest x1 13.1 us: per_device(): jnp.dot(hidden, down_matrix, preferred_element_type=jnp.float32)]
    all_to_all x1 -> x0, starting transfers between devices: 9.57 us -> none  [per_device(): lax.all_to_all(reduced.astype(jnp.bfloat16), 'ep', split_axis=0, concat_a...]
    mul x3 -> x0, other arithmetic: 4.1 us -> none  [dequant(): code_values.reshape(count_in // 32, 32, count_out) * scales[:, None, :]]
  transfers between devices with their start and end apart: 3 -> 0, of which waited for: 3 -> 0; matrix products, arithmetic and copies ran while one was open for 2% -> 0% of each run, Pallas kernels for 0% -> 0%
where the time goes in v1:
time: 71.4 us; the launch traced here: 71.3 us
  Pallas kernels  69.8 us (98%)
  local copies, waits for them, and re-layouts  1.42 us (2%)
    pallas_call x1, Pallas kernels, per_device(): pl.pallas_call(kernel, out_shape=jax.ShapeDtypeStruct((count, feat), BF),...  69.8 us

profile of v1, /device:TPU:1, one launch (start us, length us, event | category | flops | bytes accessed | tf_op | source)
XLA Modules:
  0.0 71.3 jit_solution(703668128883298248)
XLA Ops:
  0.0 69.8 %moe.1 = bf16[32,768]{1,0:T(8,128)(2,1)} custom-call(bf16[32,768]{1,0:T(8,128)(2,1)} %tokens.1, s32[2,32]{1,0:T(2,128)} %bitcast.2, f32[2,32]{1,0:T(2,128)} %bitcast.3, bf16[6144,256]{1,0:T(8,128)(2,1)} %gate_c.1, bf16[192,256]{1,0:T(8,128)(2,1)} %gate_s.1, bf16[6144,256]{1,0:T(8,128)(2,1)} %up_c.1, bf16[192,256]{1,0:T(8,128)(2,1)} %up_s.1, ...), custom_call_target="tpu_custom_call" | custom-call | tf_op jit(solution)/shard_map/moe/pallas_call | solution.py:433
  69.8 1.4 %copy.11 = bf16[32,768]{1,0:T(8,128)(2,1)} copy(bf16[32,768]{1,0:T(8,128)(2,1)} %moe.1) | data formatting | bytes 98304

commit v2 on v1

--- a/solution.py
+++ b/solution.py
@@ -19,11 +19,11 @@
 
 
 def kernel(
-    tokens, ids, combine, gate_c, gate_s, up_c, up_s, down_c, down_s,
+    tokens_in, ids_in, combine_in, gate_c, gate_s, up_c, up_s, down_c, down_s,
     out,
-    packed, X, PS, H, FIN, YB, WMAT, RA, RB, RA2, RB2,
+    tokens, ids, combine, GACC, UACC, packed, X, PS, H, FIN, YB, WMAT, RA, RB, RA2, RB2,
     GC, GS, UC, US, DC, DS,
-    wl_sem, ws_sem, wr_sem, zs_sem, zr_sem, zl_sem,
+    in_sem, wl_sem, ws_sem, wr_sem, zs_sem, zr_sem, zl_sem,
     as_sem, ar_sem, bs_sem, br_sem,
     rs_send, rs_recv, fs_sem, fr_sem,
 ):
@@ -43,6 +43,12 @@
     dev_y = {1: dev(z, ys[1], x, c), -1: dev(z, ys[3], x, c)}
     partner = dev(z, y, x, 1 - c)
 
+    inputs = []
+    for i, (src, dst) in enumerate(((ids_in, ids), (tokens_in, tokens), (combine_in, combine))):
+        copy = pltpu.make_async_copy(src, dst, in_sem.at[i])
+        copy.start()
+        inputs.append(copy)
+
     barrier = pltpu.get_barrier_semaphore()
     greeted = [partner, dev_x[1], dev_x[-1], dev_y[1], dev_y[-1]]
     for dz in range(1, NZ):
@@ -57,6 +63,9 @@
         copy = pltpu.make_async_copy(src, dst.at[0], wl_sem.at[i])
         copy.start()
         local_w.append(copy)
+
+    for copy in inputs:
+        copy.wait()
 
     count = ids.shape[1]
     slot = lax.broadcasted_iota(jnp.int32, (EXPERTS * CAP, count), 0)
@@ -81,18 +90,19 @@
 
     pl.semaphore_wait(barrier, len(greeted))
 
-    z_row = mult(y * 64 + (z // 2) * 16, 16)
+    odd = lax.rem(c + z, 2)
+    place = {0: 0, 3: 16, 1: 128, 2: 144}
     z_col = mult(x * wide + c * feat, 128)
-    z_idx = (z // 2) * 2 + c
     at_home = c == parity
     z_sends = []
-    for dz in (4, 3, 5, 2, 6, 1, 7, 0):
+    for dz in (1, 7, 2, 6, 3, 5, 4, 0):
         zt = lax.rem(z + dz, NZ)
+        k = ((NZ - dz) % NZ) // 2
         z_sends.append((dz, pltpu.make_async_remote_copy(
             src_ref=packed.at[pl.ds(mult(zt * CAP, CAP), CAP), :],
-            dst_ref=X.at[pl.ds(z_row, CAP), pl.ds(z_col, feat)],
+            dst_ref=X.at[pl.ds(mult(y * 32 + place[k], 16), CAP), pl.ds(z_col, feat)],
             send_sem=zs_sem.at[dz],
-            recv_sem=zr_sem.at[z_idx],
+            recv_sem=zr_sem.at[k * 2 + c],
             device_id=dev(zt, y, x, parity),
             device_id_type=MESH,
         )))
@@ -114,34 +124,36 @@
     def _():
         copy = pltpu.make_async_copy(
             packed.at[pl.ds(mult(z * CAP, CAP), CAP), :],
-            X.at[pl.ds(z_row, CAP), pl.ds(z_col, feat)],
+            X.at[pl.ds(mult(y * 32, 16), CAP), pl.ds(z_col, feat)],
             zl_sem,
         )
         copy.start()
         copy.wait()
 
-    def z_arrived(zi):
+    def z_arrived(k):
         for cc in range(2):
-            region = X.at[
-                pl.ds(mult(y * 64 + zi * 16, 16), CAP),
+            area = X.at[
+                pl.ds(mult(y * 32 + place[k], 16), CAP),
                 pl.ds(mult(x * wide + cc * feat, 128), feat),
             ]
             copy = pltpu.make_async_remote_copy(
-                src_ref=region, dst_ref=region, send_sem=zs_sem.at[0],
-                recv_sem=zr_sem.at[zi * 2 + cc], device_id=partner, device_id_type=MESH,
+                src_ref=area, dst_ref=area, send_sem=zs_sem.at[0],
+                recv_sem=zr_sem.at[k * 2 + cc], device_id=partner, device_id_type=MESH,
             )
-            here = jnp.logical_and(2 * zi + c == z, c == cc)
-            pl.when(jnp.logical_not(here))(copy.wait_recv)
+            if k == 0:
+                here = jnp.logical_and(odd == 0, c == cc)
+                pl.when(jnp.logical_not(here))(copy.wait_recv)
+            else:
+                copy.wait_recv()
 
     def region(ref, half, yy, xx, part):
         start, size = {None: (0, 32), 0: (0, 16), 1: (16, 16)}[part]
         return ref.at[
-            pl.ds(mult(yy * 64 + half * 32 + start, 16), size),
+            pl.ds(mult(half * 128 + yy * 32 + start, 16), size),
             pl.ds(mult(xx * wide, 128), wide),
         ]
 
     sends = []
-    SIGN = (1, -1)
 
     class Gather:
         def __init__(self, half, send_sem, recv_sem):
@@ -172,85 +184,123 @@
                 device_id=partner, device_id_type=MESH,
             ).wait_recv()
 
-        def start1(self):
-            self.send(0, 0, None, self.dev1[1], 0)
-            self.send(0, 0, None, self.dev1[-1], 1)
-
         OFF = (0, -1, 1, 2)
 
+        def begin1(self, part):
+            self.send(0, 0, part, self.dev1[1], 2 * part)
+            self.send(0, 0, part, self.dev1[-1], 2 * part + 1)
+
+        def begin2(self, part):
+            self.send(0, 0, part, self.dev2[1], 6 + 2 * part)
+            self.send(0, 0, part, self.dev2[-1], 7 + 2 * part)
+
         def start2(self, j):
-            self.send(self.OFF[j], 0, None, self.dev2[1], 4 + 4 * j)
-            self.send(self.OFF[j], 0, None, self.dev2[-1], 5 + 4 * j)
+            a, base = self.OFF[j], 6 + 6 * j
+            self.send(a, 0, 0, self.dev2[1], base)
+            self.send(a, 0, 1, self.dev2[-1], base + 3)
+            self.send(a, 0, 1, self.dev2[1], base + 2)
+            self.send(a, 0, 0, self.dev2[-1], base + 1)
 
         def pass1(self):
-            self.arrived(-1, 0, None, 0)
-            self.send(-1, 0, 0, self.dev1[1], 2)
-            self.arrived(1, 0, None, 1)
-            self.send(1, 0, 1, self.dev1[-1], 3)
+            self.arrived(-1, 0, 0, 0)
+            self.send(-1, 0, 0, self.dev1[1], 4)
+            self.arrived(1, 0, 1, 3)
+            self.send(1, 0, 1, self.dev1[-1], 5)
+            self.arrived(-1, 0, 1, 2)
+            self.arrived(1, 0, 0, 1)
 
         def end1(self):
-            self.arrived(2, 0, 0, 2)
-            self.arrived(2, 0, 1, 3)
+            self.arrived(2, 0, 0, 4)
+            self.arrived(2, 0, 1, 5)
 
         def pass2(self, j):
-            a = self.OFF[j]
-            self.arrived(a, -1, None, 4 + 4 * j)
-            self.send(a, -1, 0, self.dev2[1], 6 + 4 * j)
-            self.arrived(a, 1, None, 5 + 4 * j)
-            self.send(a, 1, 1, self.dev2[-1], 7 + 4 * j)
+            a, base = self.OFF[j], 6 + 6 * j
+            self.arrived(a, -1, 0, base)
+            self.send(a, -1, 0, self.dev2[1], base + 4)
+            self.arrived(a, 1, 1, base + 3)
+            self.send(a, 1, 1, self.dev2[-1], base + 5)
+
+        def rest2(self, j):
+            a, base = self.OFF[j], 6 + 6 * j
+            self.arrived(a, -1, 1, base + 2)
+            self.arrived(a, 1, 0, base + 1)
 
         def end2(self, j):
-            self.arrived(self.OFF[j], 2, 0, 6 + 4 * j)
-            self.arrived(self.OFF[j], 2, 1, 7 + 4 * j)
-
-    A, B = Gather(0, as_sem, ar_sem), Gather(1, bs_sem, br_sem)
-    z_arrived(0)
-    z_arrived(1)
-    A.start1()
-    z_arrived(2)
-    z_arrived(3)
-    B.start1()
-    A.start2(0)
-    B.start2(0)
-    for g in (A, B):
-        g.pass1()
-    for g in (A, B):
-        g.start2(1)
-        g.start2(2)
-    for g in (A, B):
-        g.pass2(0)
-    for g in (A, B):
-        g.end1()
-        g.start2(3)
-    for j in (1, 2, 3):
-        for g in (A, B):
-            g.pass2(j)
-    for j in range(4):
-        for g in (A, B):
-            g.end2(j)
-
-    for copy in local_w:
-        copy.wait()
-    for copy in remote_w:
-        copy.wait_recv()
+            a, base = self.OFF[j], 6 + 6 * j
+            self.arrived(a, 2, 0, base + 4)
+            self.arrived(a, 2, 1, base + 5)
 
     def scaled(codes, scales):
         rows, cols = codes.shape
         blocks = codes.reshape(rows // 32, 32, cols) * scales[:, None, :]
         return blocks.reshape(rows, cols)
 
-    deep = X.shape[1]
-    step = 1536
+    def accumulate(xx, fresh):
+        cols = pl.ds(mult(xx * wide, 128), wide)
+        scale_rows = pl.ds(mult(xx * (wide // 32), 16), wide // 32)
+        for s in range(2):
+            for codes, scales, total in ((GC, GS, GACC), (UC, US, UACC)):
+                value = jnp.dot(
+                    X[:, cols], scaled(codes[s, cols, :], scales[s, scale_rows, :]),
+                    preferred_element_type=F32,
+                )
+                total[s] = value if fresh else total[s] + value
+
+    A, B = Gather(0, as_sem, ar_sem), Gather(1, bs_sem, br_sem)
+    for k, part in ((0, 0), (3, 1)):
+        z_arrived(k)
+        A.begin1(part)
+        A.begin2(part)
+    for k, part in ((1, 0), (2, 1)):
+        z_arrived(k)
+        B.begin1(part)
+    A.pass1()
+    B.begin2(0)
+    B.begin2(1)
+    A.start2(1)
+    B.pass1()
+    B.start2(1)
+    A.end1()
+    A.start2(3)
+    A.start2(2)
+    B.pass2(0)
+    B.start2(2)
+    A.pass2(0)
+    B.end1()
+    B.pass2(1)
+    B.start2(3)
+    A.pass2(1)
+    for copy in local_w:
+        copy.wait()
+    for copy in remote_w[:4]:
+        copy.wait_recv()
+    B.rest2(0)
+    B.end2(0)
+    accumulate(xs[0], True)
+    B.pass2(2)
+    A.pass2(3)
+    A.pass2(2)
+    B.pass2(3)
+    for j in (0, 1, 3, 2):
+        A.rest2(j)
+    B.rest2(1)
+    B.end2(1)
+    accumulate(xs[3], False)
+    B.rest2(2)
+    B.end2(2)
+    accumulate(xs[1], False)
+    for j in range(4):
+        A.end2(j)
+    B.rest2(3)
+    B.end2(3)
+    accumulate(xs[2], False)
+    for copy in remote_w[4:]:
+        copy.wait_recv()
+    units = GACC.shape[2]
     for s in range(2):
-        gate = up = None
-        for k in range(deep // step):
-            rows, srows = slice(k * step, (k + 1) * step), slice(k * step // 32, (k + 1) * step // 32)
-            xk = X[:, rows]
-            g = jnp.dot(xk, scaled(GC[s, rows, :], GS[s, srows, :]), preferred_element_type=F32)
-            u = jnp.dot(xk, scaled(UC[s, rows, :], US[s, srows, :]), preferred_element_type=F32)
-            gate, up = (g, u) if gate is None else (gate + g, up + u)
-        hidden = gate / (1.0 + jnp.exp(-gate)) * up
-        H[:, s * 256:(s + 1) * 256] = hidden.astype(BF)
+        gate = GACC[s]
+        hidden = gate / (1.0 + jnp.exp(-gate)) * UACC[s]
+        H[:, s * units:(s + 1) * units] = hidden.astype(BF)
 
     def project(xx):
         piece = 512
@@ -353,31 +403,37 @@
     RB_.far1(2)
     project(xs[0])
     RB_.far1(3)
+    both = (RB_, RA_)
     for j in range(4):
-        RA_.near1(j)
-        RB_.near1(j)
-    for r in (RA_, RB_):
+        for r in both:
+            r.near1(j)
+    for r in both:
         r.own1(0)
         r.far2()
     for j in (1, 2):
-        for r in (RA_, RB_):
+        for r in both:
             r.own1(j)
-    for r in (RA_, RB_):
+    for r in both:
         r.near2()
-    for r in (RA_, RB_):
+    for r in both:
         r.own1(3)
 
     returns = []
 
-    def give_back(zi):
+    def give_back(k):
+        zt = lax.rem(z + 2 * k + odd, NZ)
         for cc in range(2):
-            src = FIN.at[pl.ds(zi * 16, 16), pl.ds(cc * feat, feat)]
+            src = FIN.at[pl.ds({0: 0, 3: 16, 1: 32, 2: 48}[k], 16), pl.ds(cc * feat, feat)]
             dst = YB.at[pl.ds(mult(z * CAP, CAP), CAP), :]
             copy = pltpu.make_async_remote_copy(
-                src_ref=src, dst_ref=dst, send_sem=fs_sem.at[zi * 2 + cc], recv_sem=fr_sem.at[z],
-                device_id=dev(2 * zi + c, y, x, cc), device_id_type=MESH,
+                src_ref=src, dst_ref=dst, send_sem=fs_sem.at[k * 2 + cc], recv_sem=fr_sem.at[z],
+                device_id=dev(zt, y, x, cc), device_id_type=MESH,
             )
-            here = jnp.logical_and(2 * zi + c == z, c == cc)
+            if k > 0:
+                copy.start()
+                returns.append((None, copy))
+                continue
+            here = jnp.logical_and(odd == 0, c == cc)
             pl.when(jnp.logical_not(here))(copy.start)
             returns.append((here, copy))
 
@@ -387,12 +443,12 @@
                 move.start()
                 move.wait()
 
-    RA_.own2()
-    give_back(0)
-    give_back(1)
     RB_.own2()
     give_back(2)
+    give_back(1)
+    RA_.own2()
     give_back(3)
+    give_back(0)
 
     for e in range(EXPERTS):
         dst = YB.at[pl.ds(e * CAP, CAP), :]
@@ -421,7 +477,10 @@
     for copy in sends:
         copy.wait_send()
     for here, copy in returns:
-        pl.when(jnp.logical_not(here))(copy.wait_send)
+        if here is None:
+            copy.wait_send()
+        else:
+            pl.when(jnp.logical_not(here))(copy.wait_send)
 
 
 def per_device(tokens, ids, combine, gate_c, gate_s, up_c, up_s, down_c, down_s):
@@ -433,9 +492,14 @@
     return pl.pallas_call(
         kernel,
         out_shape=jax.ShapeDtypeStruct((count, feat), BF),
-        in_specs=[vmem] * 3 + [hbm] * 6,
+        in_specs=[hbm] * 9,
         out_specs=vmem,
         scratch_shapes=[
+            pltpu.VMEM((count, feat), BF),
+            pltpu.VMEM((2, count), jnp.int32),
+            pltpu.VMEM((2, count), F32),
+            pltpu.VMEM((2, 256, units), F32),
+            pltpu.VMEM((2, 256, units), F32),
             pltpu.VMEM((EXPERTS * CAP, feat), BF),
             pltpu.VMEM((256, deep), BF),
             pltpu.VMEM((256, deep), BF),
@@ -453,8 +517,8 @@
             pltpu.VMEM((2,) + up_s.shape, BF),
             pltpu.VMEM((2,) + down_c.shape, BF),
             pltpu.VMEM((2,) + down_s.shape, BF),
-            dma((6,)), dma((6,)), dma((6,)), dma((8,)), dma((8,)), dma,
-            dma((20,)), dma((20,)), dma((20,)), dma((20,)),
+            dma((3,)), dma((6,)), dma((6,)), dma((6,)), dma((8,)), dma((8,)), dma,
+            dma((30,)), dma((30,)), dma((30,)), dma((30,)),
             dma((40,)), dma((40,)), dma((8,)), dma((8,)),
         ],
         compiler_params=pltpu.CompilerParams(

time: 71.4 us -> 67.7 us (0.948)
  Pallas kernels: 69.8 us -> 66.2 us
    pallas_call x1, Pallas kernels: 69.8 us -> 66.2 us  [per_device(): pl.pallas_call(kernel, out_shape=jax.ShapeDtypeStruct((count, feat), BF),...]
where the time goes in v2:
time: 67.7 us; the launch traced here: 67.6 us
  Pallas kernels  66.2 us (98%)
  local copies, waits for them, and re-layouts  1.42 us (2%)
    pallas_call x1, Pallas kernels, per_device(): pl.pallas_call(kernel, out_shape=jax.ShapeDtypeStruct((count, feat), BF),...  66.2 us
    unnamed x1, local copies, waits for them, and re-layouts  1.42 us

profile of v2, /device:TPU:1, one launch (start us, length us, event | category | flops | bytes accessed | tf_op | source)
XLA Modules:
  0.0 67.6 jit_solution(5080429297126523662)
XLA Ops:
  0.0 66.2 %moe.1 = bf16[32,768]{1,0:T(8,128)(2,1)} custom-call(bf16[32,768]{1,0:T(8,128)(2,1)} %tokens_in.1, s32[2,32]{1,0:T(2,128)} %bitcast.2, f32[2,32]{1,0:T(2,128)} %bitcast.3, bf16[6144,256]{1,0:T(8,128)(2,1)} %gate_c.1, bf16[192,256]{1,0:T(8,128)(2,1)} %gate_s.1, bf16[6144,256]{1,0:T(8,128)(2,1)} %up_c.1, bf16[192,256]{1,0:T(8,128)(2,1)} %up_s.1, ...), custom_call_target="tpu_custom_call" | custom-call | tf_op jit(solution)/shard_map/moe/pallas_call | solution.py:492
  66.2 1.4 %copy.11 = bf16[32,768]{1,0:T(8,128)(2,1)} copy(bf16[32,768]{1,0:T(8,128)(2,1)} %moe.1) | data formatting | bytes 98304

commit v3 on v2

--- a/solution.py
+++ b/solution.py
@@ -12,6 +12,25 @@
 NX, NY, NZ = 4, 4, 8
 MESH = pl.DeviceIdType.MESH
 BF, F32 = jnp.bfloat16, jnp.float32
+
+
+GATHER_ORDER = (
+    (0, 6), (0, 1), (0, 7), (0, 0), (0, 3), (0, 8), (0, 9), (0, 2), (1, 7), (1, 6),
+    (1, 1), (1, 0), (1, 8), (1, 3), (1, 9), (1, 2), (0, 4), (0, 13), (0, 19), (0, 18),
+    (0, 12), (0, 5), (0, 21), (1, 13), (1, 12), (1, 15), (1, 18), (1, 4), (1, 5), (1, 14),
+    (1, 21), (0, 22), (0, 24), (1, 10), (0, 26), (1, 20), (1, 11), (0, 16), (0, 15), (0, 25),
+    (1, 19), (0, 20), (0, 27), (1, 24), (1, 27), (1, 17), (0, 23), (1, 22), (1, 23), (0, 11),
+    (0, 17), (1, 16), (1, 26), (0, 14), (1, 25), (0, 10), (2, 0), (1, 29), (1, 28), (0, 29),
+    (0, 28), (2, 3), (2, 1), (2, 2),
+)
+REDUCE_ORDER = (
+    (2, 2), (1, 1), (1, 0), (0, 1), (0, 0), (2, 0), (0, 4), (1, 13), (0, 13), (1, 12),
+    (2, 1), (0, 5), (0, 8), (1, 5), (1, 4), (2, 3), (1, 9), (1, 8), (0, 9), (1, 3),
+    (0, 2), (1, 2), (0, 3), (1, 7), (0, 10), (1, 6), (0, 7), (1, 10), (1, 11), (1, 20),
+    (1, 16), (1, 17), (0, 6), (0, 11), (1, 14), (0, 12), (0, 20), (1, 15), (0, 16), (1, 21),
+    (0, 17), (1, 19), (1, 22), (1, 18), (0, 15), (0, 22), (0, 21), (0, 14), (0, 18), (1, 23),
+    (0, 19), (1, 24), (0, 23), (0, 24),
+)
 
 
 def mult(value, factor):
@@ -185,50 +204,43 @@
             ).wait_recv()
 
         OFF = (0, -1, 1, 2)
-
-        def begin1(self, part):
-            self.send(0, 0, part, self.dev1[1], 2 * part)
-            self.send(0, 0, part, self.dev1[-1], 2 * part + 1)
-
-        def begin2(self, part):
-            self.send(0, 0, part, self.dev2[1], 6 + 2 * part)
-            self.send(0, 0, part, self.dev2[-1], 7 + 2 * part)
-
-        def start2(self, j):
-            a, base = self.OFF[j], 6 + 6 * j
-            self.send(a, 0, 0, self.dev2[1], base)
-            self.send(a, 0, 1, self.dev2[-1], base + 3)
-            self.send(a, 0, 1, self.dev2[1], base + 2)
-            self.send(a, 0, 0, self.dev2[-1], base + 1)
-
-        def pass1(self):
-            self.arrived(-1, 0, 0, 0)
-            self.send(-1, 0, 0, self.dev1[1], 4)
-            self.arrived(1, 0, 1, 3)
-            self.send(1, 0, 1, self.dev1[-1], 5)
-            self.arrived(-1, 0, 1, 2)
-            self.arrived(1, 0, 0, 1)
-
-        def end1(self):
-            self.arrived(2, 0, 0, 4)
-            self.arrived(2, 0, 1, 5)
-
-        def pass2(self, j):
-            a, base = self.OFF[j], 6 + 6 * j
-            self.arrived(a, -1, 0, base)
-            self.send(a, -1, 0, self.dev2[1], base + 4)
-            self.arrived(a, 1, 1, base + 3)
-            self.send(a, 1, 1, self.dev2[-1], base + 5)
-
-        def rest2(self, j):
-            a, base = self.OFF[j], 6 + 6 * j
-            self.arrived(a, -1, 1, base + 2)
-            self.arrived(a, 1, 0, base + 1)
-
-        def end2(self, j):
-            a, base = self.OFF[j], 6 + 6 * j
-            self.arrived(a, 2, 0, base + 4)
-            self.arrived(a, 2, 1, base + 5)
+        CAME = {(-1, 0): 0, (1, 0): 1, (-1, 1): 2, (1, 1): 3, (2, 0): 4, (2, 1): 5}
+
+        def where(self, index):
+            ring, i = divmod(index, 6)
+            part = i - 4 if i > 3 else i // 2
+            step = (2, 2, 0, 1) if i > 3 else ((-1, 0, 1, 1), (1, 0, -1, -1))[i % 2]
+            return ring, i, part, step[0]
+
+        def go(self, index):
+            ring, i, part, _ = self.where(index)
+            up = 1 if i in (0, 2, 4) else -1
+            moved = 0 if i < 4 else -up
+            if ring == 0:
+                a, b, device = moved, 0, self.dev1[up]
+            else:
+                a, b, device = self.OFF[ring - 1], moved, self.dev2[up]
+            if i > 3:
+                self.need(index - i + (0 if i == 4 else 3))
+            elif ring > 1:
+                self.need(self.CAME[(a, part)])
+            elif a == 0 and moved == 0:
+                self.slots(part)
+            self.send(a, b, part, device, index)
+
+        def slots(self, part):
+            k = {(0, 0): 0, (0, 1): 3, (1, 0): 1, (1, 1): 2}[(self.half, part)]
+            if k not in landed:
+                landed.add(k)
+                z_arrived(k)
+
+        def need(self, index):
+            if (self.half, index) in landed:
+                return
+            landed.add((self.half, index))
+            ring, i, part, off = self.where(index)
+            a, b = (off, 0) if ring == 0 else (self.OFF[ring - 1], off)
+            self.arrived(a, b, part, index)
 
     def scaled(codes, scales):
         rows, cols = codes.shape
@@ -247,53 +259,40 @@
                 total[s] = value if fresh else total[s] + value
 
     A, B = Gather(0, as_sem, ar_sem), Gather(1, bs_sem, br_sem)
-    for k, part in ((0, 0), (3, 1)):
-        z_arrived(k)
-        A.begin1(part)
-        A.begin2(part)
-    for k, part in ((1, 0), (2, 1)):
-        z_arrived(k)
-        B.begin1(part)
-    A.pass1()
-    B.begin2(0)
-    B.begin2(1)
-    A.start2(1)
-    B.pass1()
-    B.start2(1)
-    A.end1()
-    A.start2(3)
-    A.start2(2)
-    B.pass2(0)
-    B.start2(2)
-    A.pass2(0)
-    B.end1()
-    B.pass2(1)
-    B.start2(3)
-    A.pass2(1)
-    for copy in local_w:
-        copy.wait()
-    for copy in remote_w[:4]:
-        copy.wait_recv()
-    B.rest2(0)
-    B.end2(0)
-    accumulate(xs[0], True)
-    B.pass2(2)
-    A.pass2(3)
-    A.pass2(2)
-    B.pass2(3)
-    for j in (0, 1, 3, 2):
-        A.rest2(j)
-    B.rest2(1)
-    B.end2(1)
-    accumulate(xs[3], False)
-    B.rest2(2)
-    B.end2(2)
-    accumulate(xs[1], False)
-    for j in range(4):
-        A.end2(j)
-    B.rest2(3)
-    B.end2(3)
-    accumulate(xs[2], False)
+    halves = (A, B)
+    landed = set()
+    def column(offset):
+        low, high = {0: (None, None), 3: ((0, 2), 1), 1: ((1, 3), 2), 2: ((4, 5), 3)}[offset]
+        if offset == 0:
+            for i in range(6):
+                A.need(i)
+            B.slots(0)
+            B.slots(1)
+        else:
+            for j in range(4):
+                for i in low:
+                    A.need(6 + 6 * j + i)
+            for i in low:
+                B.need(i)
+        for i in range(6):
+            B.need(6 + 6 * (high or 0) + i)
+
+    fresh = True
+    for kind, index in GATHER_ORDER:
+        if kind < 2:
+            halves[kind].go(index)
+            continue
+        if fresh:
+            for copy in local_w:
+                copy.wait()
+            for copy in remote_w[:4]:
+                copy.wait_recv()
+        column(index)
+        accumulate(xs[index], fresh)
+        fresh = False
+    for half in range(2):
+        for index in range(30):
+            halves[half].need(index)
     for copy in remote_w[4:]:
         copy.wait_recv()
     units = GACC.shape[2]
@@ -342,19 +341,21 @@
         def arrived(self, dst, index):
             self.copy(dst, dst, partner, index).wait_recv()
 
-        def far(self, pieces, buf, dev_, index):
-            self.send(pieces(2, 0), buf.at[pl.ds(64, 16)], dev_[-1], index)
-            self.send(pieces(2, 1), buf.at[pl.ds(80, 16)], dev_[1], index + 1)
-
-        def near(self, pieces, buf, dev_, index):
-            self.arrived(buf.at[pl.ds(64, 16)], index)
-            low = pieces(-1, 0)
-            low[...] = (low[...].astype(F32) + buf[64:80, :].astype(F32)).astype(BF)
-            self.send(pieces(-1, None), buf.at[pl.ds(32, 32)], dev_[-1], index + 2)
-            self.arrived(buf.at[pl.ds(80, 16)], index + 1)
-            high = pieces(1, 1)
-            high[...] = (high[...].astype(F32) + buf[80:96, :].astype(F32)).astype(BF)
-            self.send(pieces(1, None), buf.at[pl.ds(0, 32)], dev_[1], index + 3)
+        def go(self, index):
+            j, i = divmod(index, 4)
+            pieces, buf, base = self.ring1(j) if j < 4 else (self.ring2, self.R2, 16)
+            devices = self.dev1 if j < 4 else self.dev2
+            down, part = i % 2 == 0, i % 2
+            device = devices[-1 if down else 1]
+            landing = buf.at[pl.ds(64 + 16 * part, 16)]
+            if i < 2:
+                self.send(pieces(2, part), landing, device, index)
+                return
+            a = -1 if down else 1
+            self.arrived(landing, base + part)
+            mine = pieces(a, part)
+            mine[...] = (mine[...].astype(F32) + landing[...].astype(F32)).astype(BF)
+            self.send(pieces(a, None), buf.at[pl.ds(32 if down else 0, 32)], device, index)
 
         def own(self, pieces, buf, index):
             self.arrived(buf.at[pl.ds(32, 32)], index + 2)
@@ -367,14 +368,6 @@
         def ring1(self, j):
             return (lambda a, part: self.reg(a, self.OFF[j], part)), self.R1.at[j], 4 * j
 
-        def far1(self, j):
-            pieces, buf, index = self.ring1(j)
-            self.far(pieces, buf, self.dev1, index)
-
-        def near1(self, j):
-            pieces, buf, index = self.ring1(j)
-            self.near(pieces, buf, self.dev1, index)
-
         def own1(self, j):
             pieces, buf, index = self.ring1(j)
             value = self.own(pieces, buf, index)
@@ -383,40 +376,10 @@
         def ring2(self, a, part):
             return self.reg(0, a, part)
 
-        def far2(self):
-            self.far(self.ring2, self.R2, self.dev2, 16)
-
-        def near2(self):
-            self.near(self.ring2, self.R2, self.dev2, 16)
-
         def own2(self):
             FIN[self.half * 32:(self.half + 1) * 32, :] = self.own(self.ring2, self.R2, 16)
 
-    RA_, RB_ = Reduce(0, 0, RA, RA2), Reduce(1, 20, RB, RB2)
-    project(xs[2])
-    for j in range(4):
-        RA_.far1(j)
-    RB_.far1(0)
-    project(xs[1])
-    RB_.far1(1)
-    project(xs[3])
-    RB_.far1(2)
-    project(xs[0])
-    RB_.far1(3)
-    both = (RB_, RA_)
-    for j in range(4):
-        for r in both:
-            r.near1(j)
-    for r in both:
-        r.own1(0)
-        r.far2()
-    for j in (1, 2):
-        for r in both:
-            r.own1(j)
-    for r in both:
-        r.near2()
-    for r in both:
-        r.own1(3)
+    reduces = (Reduce(0, 0, RA, RA2), Reduce(1, 20, RB, RB2))
 
     returns = []
 
@@ -443,12 +406,17 @@
                 move.start()
                 move.wait()
 
-    RB_.own2()
-    give_back(2)
-    give_back(1)
-    RA_.own2()
-    give_back(3)
-    give_back(0)
+    for kind, index in REDUCE_ORDER:
+        if kind == 2:
+            project(xs[index])
+        elif index < 20:
+            reduces[kind].go(index)
+        elif index < 24:
+            reduces[kind].own1(index - 20)
+        else:
+            reduces[kind].own2()
+            for k in ((3, 0), (2, 1))[kind]:
+                give_back(k)
 
     for e in range(EXPERTS):
         dst = YB.at[pl.ds(e * CAP, CAP), :]

time: 67.7 us -> 64.6 us (0.954)
  Pallas kernels: 66.2 us -> 63.1 us
    pallas_call x1, Pallas kernels: 66.2 us -> 63.1 us  [per_device(): pl.pallas_call(kernel, out_shape=jax.ShapeDtypeStruct((count, feat), BF),...]
where the time goes in v3:
time: 64.6 us; the launch traced here: 64.5 us
  Pallas kernels  63.1 us (98%)
  local copies, waits for them, and re-layouts  1.42 us (2%)
    pallas_call x1, Pallas kernels, per_device(): pl.pallas_call(kernel, out_shape=jax.ShapeDtypeStruct((count, feat), BF),...  63.1 us
    unnamed x1, local copies, waits for them, and re-layouts  1.42 us

profile of v3, /device:TPU:1, one launch (start us, length us, event | category | flops | bytes accessed | tf_op | source)
XLA Modules:
  0.0 64.5 jit_solution(17474898108724473718)
XLA Ops:
  0.0 63.1 %moe.1 = bf16[32,768]{1,0:T(8,128)(2,1)} custom-call(bf16[32,768]{1,0:T(8,128)(2,1)} %tokens_in.1, s32[2,32]{1,0:T(2,128)} %bitcast.2, f32[2,32]{1,0:T(2,128)} %bitcast.3, bf16[6144,256]{1,0:T(8,128)(2,1)} %gate_c.1, bf16[192,256]{1,0:T(8,128)(2,1)} %gate_s.1, bf16[6144,256]{1,0:T(8,128)(2,1)} %up_c.1, bf16[192,256]{1,0:T(8,128)(2,1)} %up_s.1, ...), custom_call_target="tpu_custom_call" | custom-call | tf_op jit(solution)/shard_map/moe/pallas_call | solution.py:460
  63.1 1.4 %copy.11 = bf16[32,768]{1,0:T(8,128)(2,1)} copy(bf16[32,768]{1,0:T(8,128)(2,1)} %moe.1) | data formatting | bytes 98304

commit v4 on v3

--- a/solution.py
+++ b/solution.py
@@ -40,7 +40,7 @@
 def kernel(
     tokens_in, ids_in, combine_in, gate_c, gate_s, up_c, up_s, down_c, down_s,
     out,
-    tokens, ids, combine, GACC, UACC, packed, X, PS, H, FIN, YB, WMAT, RA, RB, RA2, RB2,
+    tokens, ids, combine, GACC, UACC, packed, X, PS, H, FIN, YB, WMAT, WHI, WLO, RA, RB, RA2, RB2,
     GC, GS, UC, US, DC, DS,
     in_sem, wl_sem, ws_sem, wr_sem, zs_sem, zr_sem, zl_sem,
     as_sem, ar_sem, bs_sem, br_sem,
@@ -69,10 +69,11 @@
         inputs.append(copy)
 
     barrier = pltpu.get_barrier_semaphore()
-    greeted = [partner, dev_x[1], dev_x[-1], dev_y[1], dev_y[-1]]
-    for dz in range(1, NZ):
+    greeted = []
+    for dz in (4, 3, 5, 2, 6, 1, 7):
         zt = lax.rem(z + dz, NZ)
         greeted += [dev(zt, y, x, c), dev(zt, y, x, 1 - c)]
+    greeted += [dev_x[1], dev_x[-1], dev_y[1], dev_y[-1], partner]
     for who in greeted:
         pl.semaphore_signal(barrier, inc=1, device_id=who, device_id_type=MESH)
 
@@ -149,6 +150,18 @@
         copy.start()
         copy.wait()
 
+    weight = WMAT[...]
+    high = weight.astype(BF)
+    low = (weight - high.astype(F32)).astype(BF)
+    slots = weight.shape[0]
+    eye = (
+        lax.broadcasted_iota(jnp.int32, (slots, slots), 0)
+        == lax.broadcasted_iota(jnp.int32, (slots, slots), 1)
+    ).astype(F32).astype(BF)
+    dims = (((0,), (0,)), ((), ()))
+    WHI[...] = lax.dot_general(high, eye, dims, preferred_element_type=F32).astype(BF)
+    WLO[...] = lax.dot_general(low, eye, dims, preferred_element_type=F32).astype(BF)
+
     def z_arrived(k):
         for cc in range(2):
             area = X.at[
@@ -418,23 +431,6 @@
             for k in ((3, 0), (2, 1))[kind]:
                 give_back(k)
 
-    for e in range(EXPERTS):
-        dst = YB.at[pl.ds(e * CAP, CAP), :]
-        copy = pltpu.make_async_remote_copy(
-            src_ref=dst, dst_ref=dst, send_sem=fs_sem.at[0], recv_sem=fr_sem.at[e],
-            device_id=partner, device_id_type=MESH,
-        )
-        here = jnp.logical_and(z == e, at_home)
-        pl.when(jnp.logical_not(here))(copy.wait_recv)
-
-    weight = WMAT[...]
-    high = weight.astype(BF)
-    low = (weight - high.astype(F32)).astype(BF)
-    dims = (((0,), (0,)), ((), ()))
-    mixed = lax.dot_general(high, YB[...], dims, preferred_element_type=F32)
-    mixed = mixed + lax.dot_general(low, YB[...], dims, preferred_element_type=F32)
-    out[...] = mixed.astype(BF)
-
     for copy in remote_w:
         copy.wait_send()
     for dz, copy in z_sends:
@@ -444,6 +440,20 @@
             copy.wait_send()
     for copy in sends:
         copy.wait_send()
+
+    for e in range(EXPERTS):
+        dst = YB.at[pl.ds(e * CAP, CAP), :]
+        copy = pltpu.make_async_remote_copy(
+            src_ref=dst, dst_ref=dst, send_sem=fs_sem.at[0], recv_sem=fr_sem.at[e],
+            device_id=partner, device_id_type=MESH,
+        )
+        here = jnp.logical_and(z == e, at_home)
+        pl.when(jnp.logical_not(here))(copy.wait_recv)
+
+    mixed = jnp.dot(WHI[...], YB[...], preferred_element_type=F32)
+    mixed = mixed + jnp.dot(WLO[...], YB[...], preferred_element_type=F32)
+    out[...] = mixed.astype(BF)
+
     for here, copy in returns:
         if here is None:
             copy.wait_send()
@@ -475,6 +485,8 @@
             pltpu.VMEM((64, wide), BF),
             pltpu.VMEM((EXPERTS * CAP, feat), BF),
             pltpu.VMEM((EXPERTS * CAP, count), F32),
+            pltpu.VMEM((count, EXPERTS * CAP), BF),
+            pltpu.VMEM((count, EXPERTS * CAP), BF),
             pltpu.VMEM((4, 96, wide), BF),
             pltpu.VMEM((4, 96, wide), BF),
             pltpu.VMEM((96, wide), BF),

time: 64.6 us -> 64.5 us (level)
  no operation moved by 1% of the time
where the time goes in v4:
time: 64.5 us; the launch traced here: 64.3 us
  Pallas kernels  62.9 us (98%)
  local copies, waits for them, and re-layouts  1.42 us (2%)
    pallas_call x1, Pallas kernels, per_device(): pl.pallas_call(kernel, out_shape=jax.ShapeDtypeStruct((count, feat), BF),...  62.9 us
    unnamed x1, local copies, waits for them, and re-layouts  1.42 us

profile of v4, /device:TPU:1, one launch (start us, length us, event | category | flops | bytes accessed | tf_op | source)
XLA Modules:
  0.0 64.3 jit_solution(3232982585531354566)
XLA Ops:
  0.0 62.9 %moe.1 = bf16[32,768]{1,0:T(8,128)(2,1)} custom-call(bf16[32,768]{1,0:T(8,128)(2,1)} %tokens_in.1, s32[2,32]{1,0:T(2,128)} %bitcast.2, f32[2,32]{1,0:T(2,128)} %bitcast.3, bf16[6144,256]{1,0:T(8,128)(2,1)} %gate_c.1, bf16[192,256]{1,0:T(8,128)(2,1)} %gate_s.1, bf16[6144,256]{1,0:T(8,128)(2,1)} %up_c.1, bf16[192,256]{1,0:T(8,128)(2,1)} %up_s.1, ...), custom_call_target="tpu_custom_call" | custom-call | tf_op jit(solution)/shard_map/moe/pallas_call | solution.py:470
  62.9 1.4 %copy.11 = bf16[32,768]{1,0:T(8,128)(2,1)} copy(bf16[32,768]{1,0:T(8,128)(2,1)} %moe.1) | data formatting | bytes 98304
